TPU v7x, 32 devices: a whole 2x2x4 slice. The times are simulated.
32 devices in a mesh: expert: 16 (over z, x, core), replica: 2 (over y).
Axes of the slice: x: 2, y: 2, z: 4, core: 2. Of those that a mesh axis runs over, the one named last changes fastest.
Arguments:
- tokens: bfloat16 [192, 3584], P('expert', 'replica'), may hold values from -6 to 6
- expert_ids: int32 [192, 8], P('expert'), may hold values from 0 to 7, all different within a row; in each aligned block of 12 rows (0 to 11, 12 to 23, ...) at most 12 rows name the same one
- gate_values: float32 [192, 8], P('expert'), may hold values from 0.1 to 0.6
- gate_weight: bfloat16 [16, 512, 3584], P('expert', 'replica'), may hold values from -0.09375 to 0.09375
- up_weight: bfloat16 [16, 512, 3584], P('expert', 'replica'), may hold values from -0.09375 to 0.09375
- down_weight: bfloat16 [16, 512, 3584], P('expert', None, 'replica'), may hold values from -0.1875 to 0.1875
- out_grad: bfloat16 [192, 3584], P('expert', 'replica'), may hold values from -1.5 to 1.5
Outputs:
- moe_out: bfloat16 [192, 3584], P('expert', 'replica')
- token_grad: bfloat16 [192, 3584], P('expert', 'replica')
- gate_grad: bfloat16 [16, 512, 3584], P('expert', 'replica')
- up_grad: bfloat16 [16, 512, 3584], P('expert', 'replica')
- down_grad: bfloat16 [16, 512, 3584], P('expert', None, 'replica')
Inputs may be any that keep to these rules, and one draw needn't show every extreme that they name: `expert_ids`: each row names 8 different experts. Among the 12 rows of one index of expert, no expert is named by more than 12 rows, a bound that some block reaches.
All inputs are finite; a program needn't handle non-finite values.
Results may differ from a plain program's by a relative error of at most 0.0075.
Values may be sent and summed in bfloat16 or wider, within the bound.
No kernel may reach another device: no remote copies, remote signals or barrier semaphores. Data moves between devices by JAX's collectives and lax.ppermute only.
A program may use at most 128 MiB of HBM per device.

v0:
```python
import jax
import jax.numpy as jnp
from jax import lax
from jax.experimental import pallas as pl
from jax.experimental.pallas import tpu as pltpu
from jax.sharding import PartitionSpec as P


BF16, F32 = jnp.bfloat16, jnp.float32
LANES = 128


def partner_2(block, axis, distance):
    count = lax.axis_size(axis)
    route = []
    for low in range(count):
        high = low | 1 << distance
        if high != low and high < count:
            route += [(low, high), (high, low)]
    return lax.ppermute(block, axis, route)


def pair_join(parity_bit, own_part, peer_part, stack_axis):
    first_part = jnp.where(parity_bit == 0, own_part, peer_part)
    second_part = jnp.where(parity_bit == 0, peer_part, own_part)
    return jnp.stack([first_part, second_part], axis=stack_axis)


def pick_half(parity_bit, stacked, stack_axis):
    lower = jnp.take(stacked, 0, axis=stack_axis)
    higher = jnp.take(stacked, 1, axis=stack_axis)
    return (jnp.where(parity_bit == 0, lower, higher), jnp.where(parity_bit == 0, higher, lower))


def routed_device(tokens, expert_ids, gate_values, gate_weight, up_weight, down_weight, out_grad):
    experts_axis = lax.axis_size("expert")
    tok_rows, slice_width = tokens.shape
    top_count = expert_ids.shape[1]
    expert_count = experts_axis // 2
    most_rows = min(tok_rows, 4 * tok_rows * top_count // (3 * expert_count))
    capacity = (most_rows + 1) // 2
    pair_count = tok_rows * top_count
    slot_count = experts_axis * capacity
    flat_ids = expert_ids.reshape(pair_count)
    onehot = (flat_ids[:, None] == jnp.arange(expert_count, dtype=jnp.int32)[None, :]).astype(
        jnp.int32
    )
    rank_in = jnp.sum((jnp.cumsum(onehot, axis=0) - onehot) * onehot, axis=1)
    upper_copy = (rank_in >= capacity).astype(jnp.int32)
    target = (2 * flat_ids + upper_copy) * capacity + rank_in - upper_copy * capacity
    slot_match = target[None, :] == jnp.arange(slot_count, dtype=jnp.int32)[:, None]
    filled = jnp.any(slot_match, axis=1)
    source_pair = jnp.sum(
        jnp.where(slot_match, jnp.arange(pair_count, dtype=jnp.int32)[None, :], 0), axis=1
    )
    source_token = source_pair // top_count
    flat_gates = gate_values.reshape(pair_count)
    send_rows = jnp.where(filled[:, None], tokens[source_token], jnp.zeros((), tokens.dtype))
    scaled = flat_gates[source_pair][:, None] * out_grad[source_token].astype(jnp.float32)
    send_grads = jnp.where(filled[:, None], scaled, 0.0).astype(jnp.bfloat16)
    got_rows, got_grads = (
        lax.all_to_all(
            send_rows.reshape(experts_axis, capacity, slice_width),
            "expert",
            split_axis=0,
            concat_axis=0,
            tiled=True,
        ),
        lax.all_to_all(
            send_grads.reshape(experts_axis, capacity, slice_width),
            "expert",
            split_axis=0,
            concat_axis=0,
            tiled=True,
        ),
    )
    rows_part = got_rows.reshape(slot_count, slice_width)
    grads_part = got_grads.reshape(slot_count, slice_width)
    parity_bit = lax.axis_index("expert") % 2
    own_pieces = (gate_weight[0], up_weight[0], down_weight[0])
    partner = partner_2((own_pieces[0], own_pieces[1], own_pieces[2]), "expert", 0)
    w_gate = pair_join(parity_bit, own_pieces[0], partner[0], 0)
    w_up = pair_join(parity_bit, own_pieces[1], partner[1], 0)
    w_down = pair_join(parity_bit, own_pieces[2], partner[2], 0)
    _, quarter, model_width = w_gate.shape
    full_rows = lax.all_gather(rows_part, "replica", axis=1, tiled=True)
    contract = (((1,), (1,)), ((), ()))
    pre_gate = lax.dot_general(
        full_rows,
        w_gate.reshape(2 * quarter, model_width),
        contract,
        preferred_element_type=jnp.float32,
    ).reshape(slot_count, 2, quarter)
    pre_up = lax.dot_general(
        full_rows,
        w_up.reshape(2 * quarter, model_width),
        contract,
        preferred_element_type=jnp.float32,
    ).reshape(slot_count, 2, quarter)
    sigma = jax.nn.sigmoid(pre_gate)
    activated = pre_gate * sigma
    slope_term = sigma * (1.0 + pre_gate * (1.0 - sigma))
    hidden = (activated * pre_up).astype(jnp.bfloat16)
    all_hidden = lax.all_gather(hidden, "replica", axis=2, tiled=True).reshape(slot_count, -1)
    down_full = w_down.reshape(-1, slice_width)
    expert_out = jnp.dot(all_hidden, down_full, preferred_element_type=jnp.float32).astype(
        jnp.bfloat16
    )
    returned = lax.all_to_all(
        expert_out.reshape(experts_axis, capacity, slice_width),
        "expert",
        split_axis=0,
        concat_axis=0,
        tiled=True,
    ).reshape(slot_count, slice_width)
    picked = returned[target].astype(jnp.float32).reshape(tok_rows, top_count, slice_width)
    moe_out = jnp.sum(picked * gate_values[:, :, None], axis=1).astype(jnp.bfloat16)
    down_local = lax.dot_general(
        all_hidden, grads_part, (((0,), (0,)), ((), ())), preferred_element_type=jnp.float32
    )
    partial_value = lax.dot_general(
        grads_part, down_full, contract, preferred_element_type=jnp.float32
    )
    hidden_grad = lax.psum_scatter(
        partial_value.reshape(slot_count, 2, -1), "replica", scatter_dimension=2, tiled=True
    )
    gate_act = (hidden_grad * pre_up * slope_term).astype(jnp.bfloat16)
    up_act = (hidden_grad * activated).astype(jnp.bfloat16)
    gate_local = jnp.einsum("sd,shq->hqd", full_rows, gate_act, preferred_element_type=jnp.float32)
    up_local = jnp.einsum("sd,shq->hqd", full_rows, up_act, preferred_element_type=jnp.float32)
    all_gate_act, all_up_act = (
        lax.all_gather(gate_act, "replica", axis=2, tiled=True),
        lax.all_gather(up_act, "replica", axis=2, tiled=True),
    )
    rows_gate, rows_up = (
        lax.all_to_all(w_gate, "replica", split_axis=2, concat_axis=1, tiled=True),
        lax.all_to_all(w_up, "replica", split_axis=2, concat_axis=1, tiled=True),
    )
    input_rows = jnp.einsum(
        "shf,hfd->sd", all_gate_act, rows_gate, preferred_element_type=jnp.float32
    )
    input_rows = input_rows + jnp.einsum(
        "shf,hfd->sd", all_up_act, rows_up, preferred_element_type=jnp.float32
    )
    grads_back = lax.all_to_all(
        input_rows.astype(jnp.bfloat16).reshape(experts_axis, capacity, slice_width),
        "expert",
        split_axis=0,
        concat_axis=0,
        tiled=True,
    ).reshape(slot_count, slice_width)
    token_grad = jnp.sum(
        grads_back[target].astype(jnp.float32).reshape(tok_rows, top_count, slice_width), axis=1
    ).astype(jnp.bfloat16)
    keep_gate, give_gate = pick_half(parity_bit, gate_local, 0)
    keep_up, give_up = pick_half(parity_bit, up_local, 0)
    keep_down, give_down = pick_half(parity_bit, down_local.reshape(2, -1, slice_width), 0)
    received = (
        partner_2(give_gate.astype(jnp.bfloat16), "expert", 0).astype(give_gate.dtype),
        partner_2(give_up.astype(jnp.bfloat16), "expert", 0).astype(give_up.dtype),
        partner_2(give_down.astype(jnp.bfloat16), "expert", 0).astype(give_down.dtype),
    )
    gate_grad = (keep_gate + received[0]).astype(jnp.bfloat16)[None]
    up_grad = (keep_up + received[1]).astype(jnp.bfloat16)[None]
    down_grad = (keep_down + received[2]).astype(jnp.bfloat16)[None]
    return (moe_out, token_grad, gate_grad, up_grad, down_grad)


def dot(left, right, dims):
    return lax.dot_general(left, right, (dims, ((), ())), preferred_element_type=F32)


def gate_column(place, tables):
    table = jnp.concatenate([ref[:, -LANES:] for ref in tables], axis=0).astype(F32)
    lane = lax.broadcasted_iota(jnp.int32, table.shape, 1)
    count = place[3]
    mine = (lane == place[2]) | (lane == place[2] + count) | (lane == place[2] + 2 * count)
    return jnp.sum(jnp.where(mine, table, 0.0), axis=1, keepdims=True)


def columns(index, width):
    return pl.ds(pl.multiple_of(index * width, width), width)


def load_kernel(place, gate_hbm, up_hbm, down_hbm, gate, up, down, sems):
    copies = [pltpu.make_async_copy(source, target, sems.at[n])
              for n, (source, target) in enumerate(
                  ((down_hbm, down), (gate_hbm, gate), (up_hbm, up)))]
    for copy in copies:
        copy.start()
    for copy in copies:
        copy.wait()


def cotangent_kernel(place, og00, og01, og10, og11, down, keep, give):
    width, units = og10.shape[1], keep.shape[1]
    total = [None, None]
    for c_rel, parts in enumerate(((og00, og01), (og10, og11))):
        rows = jnp.concatenate([part[:, :width] for part in parts], axis=0)
        for r_rel in range(2):
            block = down[columns(place[0] ^ r_rel, units), columns(place[1] ^ c_rel, width)]
            term = dot(rows, block, ((1,), (1,)))
            total[r_rel] = term if total[r_rel] is None else total[r_rel] + term
    keep[...] = total[0]
    give[...] = total[1].astype(give.dtype)


def hidden_kernel(place, x000, x001, x010, x011, x100, x101, x110, x111, t0, t1, gate, up,
                  hidden, act, slope):
    width = x000.shape[1]
    a = b = None
    for r_rel, c_rel, parts in ((0, 0, (x000, x001)), (0, 1, (x010, x011)),
                                (1, 0, (x100, x101)), (1, 1, (x110, x111))):
        rows = jnp.concatenate([part[...] for part in parts], axis=0)
        where = columns((place[0] ^ r_rel) * 2 + (place[1] ^ c_rel), width)
        term_a = dot(rows, gate[:, where], ((1,), (1,)))
        term_b = dot(rows, up[:, where], ((1,), (1,)))
        a = term_a if a is None else a + term_a
        b = term_b if b is None else b + term_b
    weight = gate_column(place, (t0, t1))
    sigma = jax.nn.sigmoid(a)
    silu = a * sigma
    hidden[...] = (weight * (silu * b)).astype(hidden.dtype)
    act[...] = weight * silu
    slope[...] = weight * (b * (sigma * (1.0 + a * (1.0 - sigma))))


def input_kernel(place, own, other, act, slope, gate, up, da_out, db_out, keep, give):
    width = keep.shape[2]
    dh = own[...] + other[...].astype(F32)
    da = (dh * slope[...]).astype(BF16)
    db = (dh * act[...]).astype(BF16)
    da_out[...] = da
    db_out[...] = db
    for r_rel in range(2):
        for c_rel in range(2):
            where = columns((place[0] ^ r_rel) * 2 + (place[1] ^ c_rel), width)
            block = dot(da, gate[:, where], ((1,), (0,))) + dot(db, up[:, where], ((1,), (0,)))
            if c_rel == 0:
                keep[r_rel] = block
            else:
                give[r_rel] = block.astype(give.dtype)


def output_kernel(place, own, other, down, keep, give):
    width, units = keep.shape[1], own.shape[1]
    for c_rel in range(2):
        where = columns(place[1] ^ c_rel, width)
        block = dot(own[...], down[columns(place[0], units), where], ((1,), (0,)))
        block = block + dot(other[...], down[columns(place[0] ^ 1, units), where], ((1,), (0,)))
        if c_rel == 0:
            keep[...] = block
        else:
            give[...] = block.astype(give.dtype)


def down_grad_kernel(place, own, other, og00, og01, og10, og11, down_grad):
    width, units = og10.shape[1], own.shape[1]
    for c_rel, parts in enumerate(((og00, og01), (og10, og11))):
        rows = jnp.concatenate([part[:, :width] for part in parts], axis=0)
        for r_rel, hidden in ((0, own), (1, other)):
            block = dot(hidden[...], rows, ((0,), (0,)))
            down_grad[columns(place[0] ^ r_rel, units), columns(place[1] ^ c_rel, width)] = (
                block.astype(down_grad.dtype)
            )


def weight_grad_kernel(place, da, db, x000, x001, x010, x011, x100, x101, x110, x111,
                       gate_grad, up_grad):
    width = x000.shape[1]
    for r_rel, c_rel, parts in ((0, 0, (x000, x001)), (0, 1, (x010, x011)),
                                (1, 0, (x100, x101)), (1, 1, (x110, x111))):
        rows = jnp.concatenate([part[...] for part in parts], axis=0)
        where = columns((place[0] ^ r_rel) * 2 + (place[1] ^ c_rel), width)
        gate_grad[:, where] = dot(da[...], rows, ((0,), (0,))).astype(gate_grad.dtype)
        up_grad[:, where] = dot(db[...], rows, ((0,), (0,))).astype(up_grad.dtype)


def call(kernel, place, operands, outs, flops, in_hbm=(), scratch=(), limit=24 << 20):
    moved = sum(x.size * x.dtype.itemsize for x in (*operands, *outs))
    vmem = pl.BlockSpec(memory_space=pltpu.VMEM)
    hbm = pl.BlockSpec(memory_space=pltpu.HBM)
    return pl.pallas_call(
        kernel,
        out_shape=list(outs),
        in_specs=[pl.BlockSpec(memory_space=pltpu.SMEM)]
        + [hbm if n in in_hbm else vmem for n in range(len(operands))],
        out_specs=[vmem] * len(outs),
        scratch_shapes=list(scratch),
        compiler_params=pltpu.CompilerParams(vmem_limit_bytes=limit),
        cost_estimate=pl.CostEstimate(flops=flops, bytes_accessed=moved, transcendentals=0),
    )(place, *operands)


def struct(shape, dtype):
    return jax.ShapeDtypeStruct(shape, dtype)


def swap(value, expert_bits, replica_bit=0):
    count, replicas = lax.axis_size("expert"), lax.axis_size("replica")
    flip = expert_bits * replicas + replica_bit
    if not replica_bit:
        return lax.ppermute(value, "expert", [(i, i ^ expert_bits) for i in range(count)])
    if not expert_bits:
        return lax.ppermute(value, "replica", [(i, i ^ flip) for i in range(replicas)])
    return lax.ppermute(
        value, ("expert", "replica"), [(i, i ^ flip) for i in range(count * replicas)]
    )


def dense_device(tokens, expert_ids, gate_values, gate_weight, up_weight, down_weight, out_grad):
    devices = lax.axis_size("expert")
    experts, far = devices // 2, devices // 4
    tok_rows, slice_width = tokens.shape
    half = slice_width // 2
    me = lax.axis_index("expert")
    core, replica = me % 2, lax.axis_index("replica")
    place = jnp.stack([replica, core, me // 2, jnp.int32(experts)]).astype(jnp.int32)
    gate, up, down = gate_weight[0], up_weight[0], down_weight[0]
    units, model_width = gate.shape

    def order(own, peer, axis):
        return jnp.where(
            core == 0,
            jnp.concatenate([own, peer], axis=axis),
            jnp.concatenate([peer, own], axis=axis),
        )

    routed = expert_ids[:, :, None] == jnp.arange(experts, dtype=jnp.int32)
    table = jnp.sum(jnp.where(routed, gate_values[:, :, None], 0.0), axis=1)
    parts = []
    for _ in range(3):
        part = lax.reduce_precision(table, 8, 7)
        parts.append(part.astype(BF16))
        table = table - part
    coded = jnp.concatenate(parts, axis=1)
    coded = jnp.pad(coded, ((0, 0), (0, -coded.shape[1] % LANES)))
    own = lax.optimization_barrier(jnp.concatenate([tokens, out_grad], axis=1))
    low = jnp.concatenate([own[:, :half], own[:, 2 * half : 3 * half], coded], axis=1)
    high = jnp.concatenate([own[:, half : 2 * half], own[:, 3 * half :], coded], axis=1)
    mine, theirs = jnp.where(core == 0, low, high), jnp.where(core == 0, high, low)
    gate, up, down = call(
        load_kernel, place, (gate, up, down),
        [struct(w.shape, w.dtype) for w in (gate, up, down)], 0, in_hbm=(0, 1, 2),         scratch=[pltpu.SemaphoreType.DMA((3,))],
    )
    block = order(mine, swap(theirs, 1), 0)
    got = {step: swap(block, 4 * step) for step in reversed(range(1, far))}
    blocks = [block] + [got[step] for step in range(1, far)]
    og_here = jnp.concatenate([part[:, half:] for part in blocks], axis=0)
    x_here = jnp.concatenate([part[:, :half] for part in blocks], axis=0)
    og_side = swap(og_here, 2)
    x_side = swap(x_here, 2)
    x_cross = swap(x_here, 2, 1)
    x_up = swap(x_here, 0, 1)
    og = [og_here, og_side,
          swap(og_here[:, :half], 1), swap(og_side[:, :half], 1)]
    x = [x_here, x_side, swap(x_here, 1), swap(x_side, 1),
         x_up, x_cross, swap(x_up, 1), swap(x_cross, 1)]
    side_rows = x_here.shape[0]
    all_rows = 2 * side_rows
    work = 2 * all_rows * units

    d_own, d_give = call(
        cotangent_kernel, place, (*og, down),
        (struct((all_rows, units), F32), struct((all_rows, units), BF16)),
        work * 2 * slice_width,
    )
    d_got = swap(d_give, 0, 1)
    hidden, act, slope = call(
        hidden_kernel, place, (*x, og_here, og_side, gate, up),
        (struct((all_rows, units), BF16), struct((all_rows, units), F32),
         struct((all_rows, units), F32)),
        work * 2 * model_width,
    )
    hidden_got = swap(hidden, 0, 1)
    da, db, dx_keep, dx_give = call(
        input_kernel, place, (d_own, d_got, act, slope, gate, up),
        (struct((all_rows, units), BF16), struct((all_rows, units), BF16),
         struct((2, all_rows, half), F32), struct((2, all_rows, half), BF16)),
        work * 2 * model_width,
    )
    dx = dx_keep + swap(dx_give, 1).astype(F32)
    dx_cross = swap(dx[1, side_rows:].astype(BF16), 2, 1)
    dx_side = swap(dx[0, side_rows:].astype(BF16), 2)
    dx_up = swap(dx[1, :side_rows].astype(BF16), 0, 1)

    y_keep, y_give = call(
        output_kernel, place, (hidden, hidden_got, down),
        (struct((all_rows, half), F32), struct((all_rows, half), BF16)),
        work * 2 * slice_width,
    )
    y = y_keep + swap(y_give, 1).astype(F32)
    y_side = swap(y[side_rows:].astype(BF16), 2)
    (down_grad,) = call(
        down_grad_kernel, place, (hidden, hidden_got, *og),
        (struct(down.shape, BF16),), work * 2 * slice_width,
    )
    gate_grad, up_grad = call(
        weight_grad_kernel, place, (da, db, *x),
        (struct(gate.shape, BF16), struct(up.shape, BF16)), work * 2 * model_width,
    )

    dx_sum = (dx[0, :side_rows] + dx_side.astype(F32)) + (dx_up.astype(F32) + dx_cross.astype(F32))
    y_sum = y[:side_rows] + y_side.astype(F32)
    both = jnp.concatenate([y_sum, dx_sum], axis=1)
    pair = 2 * tok_rows
    total = both[:pair]
    for step in reversed(range(1, far)):
        part = both[step * pair : (step + 1) * pair].astype(BF16)
        total = total + swap(part, 4 * step).astype(F32)
    total = total.astype(BF16)
    first, second = total[:tok_rows], total[tok_rows:]
    kept = jnp.where(core == 0, first, second)
    got = swap(jnp.where(core == 0, second, first), 1)
    moe_out = order(kept[:, :half], got[:, :half], 1)
    token_grad = order(kept[:, half:], got[:, half:], 1)
    return moe_out, token_grad, gate_grad[None], up_grad[None], down_grad[None]


def per_device(tokens, expert_ids, gate_values, gate_weight, up_weight, down_weight, out_grad):
    args = (tokens, expert_ids, gate_values, gate_weight, up_weight, down_weight, out_grad)
    devices, replicas = lax.axis_size("expert"), lax.axis_size("replica")
    every_expert = expert_ids.shape[1] == devices // 2
    power = devices & (devices - 1) == 0 and devices >= 4 and 3 * (devices // 2) <= LANES
    aligned = tokens.shape[1] % (2 * LANES) == 0 and gate_weight.shape[1] % LANES == 0
    if every_expert and power and replicas == 2 and aligned:
        return dense_device(*args)
    return routed_device(*args)


def solution(mesh):
    placed = (
        P("expert", "replica"),
        P("expert", None),
        P("expert", None),
        P("expert", "replica", None),
        P("expert", "replica", None),
        P("expert", None, "replica"),
        P("expert", "replica"),
    )
    return jax.shard_map(
        per_device,
        mesh=mesh,
        in_specs=placed,
        out_specs=(
            P("expert", "replica"),
            P("expert", "replica"),
            P("expert", "replica", None),
            P("expert", "replica", None),
            P("expert", None, "replica"),
        ),
        check_vma=False,
    )
```

profile of v0, /device:TPU:0, one launch (start us, length us, event | category | flops | bytes accessed | tf_op | source)
XLA Modules:
  0.0 74.5 jit_solution(757903311267841298)
XLA Ops:
  4.2 5.0 %collective-permute-start.3 = (bf16[24,1920]{1,0:T(8,128)(2,1)S(1)}, bf16[24,1920]{1,0:T(8,128)(2,1)S(1)}, u32[]{:S(2)}, u32[]{:S(2)}) collective-permute-start(bf16[24,1920]{1,0:T(8,128)(2,1)S(1)} %maximum_select_fusion), channel_id=1, source_target_pairs={{0,24},{2,26},{4,28},{6,30},{8,16},{10,18},{12,20},{14,22},{16,8},... | collective-permute-start | bytes 276488 | tf_op jit(solution)/shard_map/ppermute | solution.py:303
  9.9 3.0 %collective-permute-done.3 = bf16[24,1920]{1,0:T(8,128)(2,1)S(1)} collective-permute-done((bf16[24,1920]{1,0:T(8,128)(2,1)S(1)}, bf16[24,1920]{1,0:T(8,128)(2,1)S(1)}, u32[]{:S(2)}, u32[]{:S(2)}) %collective-permute-start.3) | collective-permute-done | bytes 92192 | tf_op jit(solution)/shard_map/ppermute | solution.py:303
  12.8 4.4 %collective-permute-done.2 = bf16[24,1920]{1,0:T(8,128)(2,1)S(1)} collective-permute-done((bf16[24,1920]{1,0:T(8,128)(2,1)S(1)}, bf16[24,1920]{1,0:T(8,128)(2,1)S(1)}, u32[]{:S(2)}, u32[]{:S(2)}) %collective-permute-start.2) | collective-permute-done | bytes 92192 | tf_op jit(solution)/shard_map/ppermute | solution.py:303
  17.3 1.6 %collective-permute-start.11 = (bf16[96,1024]{1,0:T(8,128)(2,1)S(1)}, bf16[96,1024]{1,0:T(8,128)(2,1)S(1)}, u32[]{:S(2)}, u32[]{:S(2)}) collective-permute-start(bf16[96,1024]{1,0:T(8,128)(2,1)S(1)} %pad_maximum_fusion.1.t0.og00), channel_id=1, source_target_pairs={{0,4},{2,6},{4,0},{6,2},{8,12},{10,14},{12,8},{14,10},{16,20},{18,... | collective-permute-start | bytes 589832 | tf_op jit(solution)/shard_map/ppermute | solution.py:303
  19.5 1.5 %collective-permute-start.7 = (bf16[96,896]{1,0:T(8,128)(2,1)S(1)}, bf16[96,896]{1,0:T(8,128)(2,1)S(1)}, u32[]{:S(2)}, u32[]{:S(2)}) collective-permute-start(bf16[96,896]{1,0:T(8,128)(2,1)S(1)} %pad_maximum_fusion.2.x000), channel_id=1, source_target_pairs={{0,1},{1,0},{2,3},{3,2},{4,5},{5,4},{6,7},{7,6},{8,9},{9,8},{10,11... | collective-permute-start | bytes 516104 | tf_op jit(solution)/shard_map/ppermute | solution.py:305
  21.0 1.4 %collective-permute-start.8 = (bf16[96,896]{1,0:T(8,128)(2,1)S(1)}, bf16[96,896]{1,0:T(8,128)(2,1)S(1)}, u32[]{:S(2)}, u32[]{:S(2)}) collective-permute-start(bf16[96,896]{1,0:T(8,128)(2,1)S(1)} %pad_maximum_fusion.2.x000), channel_id=1, source_target_pairs={{0,5},{1,4},{2,7},{3,6},{4,1},{5,0},{6,3},{7,2},{8,13},{9,12},{10,... | collective-permute-start | bytes 516104 | tf_op jit(solution)/shard_map/ppermute | solution.py:306
  23.2 2.0 %collective-permute-done.11.t1.og01 = bf16[96,1024]{1,0:T(8,128)(2,1)S(1)} collective-permute-done((bf16[96,1024]{1,0:T(8,128)(2,1)S(1)}, bf16[96,1024]{1,0:T(8,128)(2,1)S(1)}, u32[]{:S(2)}, u32[]{:S(2)}) %collective-permute-start.11) | collective-permute-done | bytes 196640 | tf_op jit(solution)/shard_map/ppermute | solution.py:303
  25.3 3.6 %collective-permute-done.4.x001 = bf16[96,896]{1,0:T(8,128)(2,1)S(1)} collective-permute-done((bf16[96,896]{1,0:T(8,128)(2,1)S(1)}, bf16[96,896]{1,0:T(8,128)(2,1)S(1)}, u32[]{:S(2)}, u32[]{:S(2)}) %collective-permute-start.4) | collective-permute-done | bytes 172064 | tf_op jit(solution)/shard_map/ppermute | solution.py:303
  29.4 2.5 %collective-permute-done.8.x101 = bf16[96,896]{1,0:T(8,128)(2,1)S(1)} collective-permute-done((bf16[96,896]{1,0:T(8,128)(2,1)S(1)}, bf16[96,896]{1,0:T(8,128)(2,1)S(1)}, u32[]{:S(2)}, u32[]{:S(2)}) %collective-permute-start.8) | collective-permute-done | bytes 172064 | tf_op jit(solution)/shard_map/ppermute | solution.py:306
  32.4 1.5 %copy-done.1 = bf16[1,256,3584]{2,1,0:T(8,128)(2,1)S(1)} copy-done((bf16[1,256,3584]{2,1,0:T(8,128)(2,1)S(1)}, bf16[1,256,3584]{2,1,0:T(8,128)(2,1)}, u32[]{:S(2)}) %copy-start.1) | copy-done | bytes 1835032
  33.9 1.5 %copy-done.2 = bf16[1,512,1792]{2,1,0:T(8,128)(2,1)S(1)} copy-done((bf16[1,512,1792]{2,1,0:T(8,128)(2,1)S(1)}, bf16[1,512,1792]{2,1,0:T(8,128)(2,1)}, u32[]{:S(2)}) %copy-start.2) | copy-done | bytes 1835032
  38.3 2.0 %shard_map.111 = (bf16[192,256]{1,0:T(8,128)(2,1)S(1)}, f32[192,256]{1,0:T(8,128)S(1)}, f32[192,256]{1,0:T(8,128)S(1)}) custom-call(s32[4]{0:T(128)S(1)} %pad_add_fusion.place, bf16[96,896]{1,0:T(8,128)(2,1)S(1)} %pad_maximum_fusion.2.x000, bf16[96,896]{1,0:T(8,128)(2,1)S(1)} %collective-permute-done.4.x001, ...), custom_call_target="tpu_custom_call" | custom-call | flops 704643072 | bytes 5931008 | tf_op jit(solution)/shard_map/pallas_call | solution.py:283
  40.3 1.6 %collective-permute-start.12 = (bf16[192,256]{1,0:T(8,128)(2,1)S(1)}, bf16[192,256]{1,0:T(8,128)(2,1)S(1)}, u32[]{:S(2)}, u32[]{:S(2)}) collective-permute-start(bf16[192,256]{1,0:T(8,128)(2,1)S(1)} %get-tuple-element.23.own), channel_id=1, source_target_pairs={{0,1},{1,0},{2,3},{3,2},{4,5},{5,4},{6,7},{7,6},{8,9},{9,8},{10,11... | collective-permute-start | bytes 294920 | tf_op jit(solution)/shard_map/ppermute | solution.py:305
  42.5 1.5 %shard_map.114 = (bf16[192,256]{1,0:T(8,128)(2,1)S(1)}, bf16[192,256]{1,0:T(8,128)(2,1)S(1)}, f32[2,192,896]{2,1,0:T(8,128)S(1)}, bf16[2,192,896]{2,1,0:T(8,128)(2,1)S(1)}) custom-call(s32[4]{0:T(128)S(1)} %pad_add_fusion.place, f32[192,256]{1,0:T(8,128)S(1)} %get-tuple-element.27.own, bf16[192,256]{1,0:T(8,128)(2,1)S(1)} %collective-permute-done.17.other, ...), custom_call_target="tpu_custom_call" | custom-call | flops 704643072 | bytes 6619136 | tf_op jit(solution)/shard_map/pallas_call | solution.py:283
  46.2 1.6 %collective-permute-done.13 = bf16[192,896]{1,0:T(8,128)(2,1)S(1)} collective-permute-done((bf16[192,896]{1,0:T(8,128)(2,1)S(1)}, bf16[192,896]{1,0:T(8,128)(2,1)S(1)}, u32[]{:S(2)}, u32[]{:S(2)}) %collective-permute-start.13) | collective-permute-done | bytes 344096 | tf_op jit(solution)/shard_map/ppermute | solution.py:303
  47.9 1.6 %collective-permute-start.14 = (bf16[96,896]{1,0:T(8,128)(2,1)S(1)}, bf16[96,896]{1,0:T(8,128)(2,1)S(1)}, u32[]{:S(2)}, u32[]{:S(2)}) collective-permute-start(bf16[96,896]{1,0:T(8,128)(2,1)S(1)} %slice.186), channel_id=1, source_target_pairs={{0,4},{2,6},{4,0},{6,2},{8,12},{10,14},{12,8},{14,10},{16,20},{18,... | collective-permute-start | bytes 516104 | tf_op jit(solution)/shard_map/ppermute | solution.py:303
  49.7 1.6 %collective-permute-start.21 = (bf16[96,896]{1,0:T(8,128)(2,1)S(1)}, bf16[96,896]{1,0:T(8,128)(2,1)S(1)}, u32[]{:S(2)}, u32[]{:S(2)}) collective-permute-start(bf16[96,896]{1,0:T(8,128)(2,1)S(1)} %get-tuple-element.40), channel_id=1, source_target_pairs={{0,5},{1,4},{2,7},{3,6},{4,1},{5,0},{6,3},{7,2},{8,13},{9,12},{10,... | collective-permute-start | bytes 516104 | tf_op jit(solution)/shard_map/ppermute | solution.py:306
  51.7 1.5 %collective-permute-start.19 = (bf16[96,896]{1,0:T(8,128)(2,1)S(1)}, bf16[96,896]{1,0:T(8,128)(2,1)S(1)}, u32[]{:S(2)}, u32[]{:S(2)}) collective-permute-start(bf16[96,896]{1,0:T(8,128)(2,1)S(1)} %get-tuple-element.39), channel_id=1, source_target_pairs={{0,4},{2,6},{4,0},{6,2},{8,12},{10,14},{12,8},{14,10},{16,20},{18,... | collective-permute-start | bytes 516104 | tf_op jit(solution)/shard_map/ppermute | solution.py:303
  53.2 2.0 %collective-permute-done.14 = bf16[96,896]{1,0:T(8,128)(2,1)S(1)} collective-permute-done((bf16[96,896]{1,0:T(8,128)(2,1)S(1)}, bf16[96,896]{1,0:T(8,128)(2,1)S(1)}, u32[]{:S(2)}, u32[]{:S(2)}) %collective-permute-start.14) | collective-permute-done | bytes 172064 | tf_op jit(solution)/shard_map/ppermute | solution.py:303
  55.3 4.7 %collective-permute-done.21 = bf16[96,896]{1,0:T(8,128)(2,1)S(1)} collective-permute-done((bf16[96,896]{1,0:T(8,128)(2,1)S(1)}, bf16[96,896]{1,0:T(8,128)(2,1)S(1)}, u32[]{:S(2)}, u32[]{:S(2)}) %collective-permute-start.21) | collective-permute-done | bytes 172064 | tf_op jit(solution)/shard_map/ppermute | solution.py:306
  62.7 2.4 %collective-permute-start.23 = (bf16[24,1792]{1,0:T(8,128)(2,1)S(1)}, bf16[24,1792]{1,0:T(8,128)(2,1)S(1)}, u32[]{:S(2)}, u32[]{:S(2)}) collective-permute-start(bf16[24,1792]{1,0:T(8,128)(2,1)S(1)} %get-tuple-element.44), channel_id=1, source_target_pairs={{0,16},{2,18},{4,20},{6,22},{8,24},{10,26},{12,28},{14,30},{16,0},... | collective-permute-start | bytes 258056 | tf_op jit(solution)/shard_map/ppermute | solution.py:303
  65.1 1.3 %collective-permute-start.22 = (bf16[24,1792]{1,0:T(8,128)(2,1)S(1)}, bf16[24,1792]{1,0:T(8,128)(2,1)S(1)}, u32[]{:S(2)}, u32[]{:S(2)}) collective-permute-start(bf16[24,1792]{1,0:T(8,128)(2,1)S(1)} %get-tuple-element.42), channel_id=1, source_target_pairs={{0,24},{2,26},{4,28},{6,30},{8,16},{10,18},{12,20},{14,22},{16,8},... | collective-permute-start | bytes 258056 | tf_op jit(solution)/shard_map/ppermute | solution.py:303
  66.4 2.5 %shard_map.116 = bf16[512,1792]{1,0:T(8,128)(2,1)} custom-call(s32[4]{0:T(128)S(1)} %pad_add_fusion.place, bf16[192,256]{1,0:T(8,128)(2,1)S(1)} %get-tuple-element.23.own, bf16[192,256]{1,0:T(8,128)(2,1)S(1)} %collective-permute-done.12.other, bf16[96,1024]{1,0:T(8,128)(2,1)S(1)} %pad_maximum_fusion.1.t0.og00, ...), custom_call_target="tpu_custom_call" | custom-call | flops 352321536 | bytes 2768896 | tf_op jit(solution)/shard_map/pallas_call | solution.py:283
  68.9 3.5 %shard_map.115 = (bf16[256,3584]{1,0:T(8,128)(2,1)}, bf16[256,3584]{1,0:T(8,128)(2,1)}) custom-call(s32[4]{0:T(128)S(1)} %pad_add_fusion.place, bf16[192,256]{1,0:T(8,128)(2,1)S(1)} %get-tuple-element.33.da, bf16[192,256]{1,0:T(8,128)(2,1)S(1)} %get-tuple-element.34.db, bf16[96,896]{1,0:T(8,128)(2,1)S(1)} %pad_maximum_fusion.2.x000, ...), custom_call_target="tpu_custom_call" | custom-call | flops 704643072 | bytes 5242880 | tf_op jit(solution)/shard_map/pallas_call | solution.py:283
  (77 shorter events, 17.9 us)
Async XLA Ops:
  4.2 8.6 %collective-permute-start.3 = (bf16[24,1920]{1,0:T(8,128)(2,1)S(1)}, bf16[24,1920]{1,0:T(8,128)(2,1)S(1)}, u32[]{:S(2)}, u32[]{:S(2)}) collective-permute-start(bf16[24,1920]{1,0:T(8,128)(2,1)S(1)} %maximum_select_fusion), channel_id=1, source_target_pairs={{0,24},{2,26},{4,28},{6,30},{8,16},{10,18},{12,20},{14,22},{16,8},... | collective-permute-start | bytes 276488 | tf_op jit(solution)/shard_map/ppermute | solution.py:303
  9.2 8.1 %collective-permute-start.2 = (bf16[24,1920]{1,0:T(8,128)(2,1)S(1)}, bf16[24,1920]{1,0:T(8,128)(2,1)S(1)}, u32[]{:S(2)}, u32[]{:S(2)}) collective-permute-start(bf16[24,1920]{1,0:T(8,128)(2,1)S(1)} %maximum_select_fusion), channel_id=1, source_target_pairs={{0,16},{2,18},{4,20},{6,22},{8,24},{10,26},{12,28},{14,30},{16,0},... | collective-permute-start | bytes 276488 | tf_op jit(solution)/shard_map/ppermute | solution.py:303
  9.2 8.1 %collective-permute-start.1 = (bf16[24,1920]{1,0:T(8,128)(2,1)S(1)}, bf16[24,1920]{1,0:T(8,128)(2,1)S(1)}, u32[]{:S(2)}, u32[]{:S(2)}) collective-permute-start(bf16[24,1920]{1,0:T(8,128)(2,1)S(1)} %maximum_select_fusion), channel_id=1, source_target_pairs={{0,8},{2,10},{4,12},{6,14},{8,0},{10,2},{12,4},{14,6},{16,24},{18,... | collective-permute-start | bytes 276488 | tf_op jit(solution)/shard_map/ppermute | solution.py:303
  17.3 7.8 %collective-permute-start.11 = (bf16[96,1024]{1,0:T(8,128)(2,1)S(1)}, bf16[96,1024]{1,0:T(8,128)(2,1)S(1)}, u32[]{:S(2)}, u32[]{:S(2)}) collective-permute-start(bf16[96,1024]{1,0:T(8,128)(2,1)S(1)} %pad_maximum_fusion.1.t0.og00), channel_id=1, source_target_pairs={{0,4},{2,6},{4,0},{6,2},{8,12},{10,14},{12,8},{14,10},{16,20},{18,... | collective-permute-start | bytes 589832 | tf_op jit(solution)/shard_map/ppermute | solution.py:303
  18.9 9.9 %collective-permute-start.4 = (bf16[96,896]{1,0:T(8,128)(2,1)S(1)}, bf16[96,896]{1,0:T(8,128)(2,1)S(1)}, u32[]{:S(2)}, u32[]{:S(2)}) collective-permute-start(bf16[96,896]{1,0:T(8,128)(2,1)S(1)} %pad_maximum_fusion.2.x000), channel_id=1, source_target_pairs={{0,4},{2,6},{4,0},{6,2},{8,12},{10,14},{12,8},{14,10},{16,20},{18,... | collective-permute-start | bytes 516104 | tf_op jit(solution)/shard_map/ppermute | solution.py:303
  19.5 9.3 %collective-permute-start.7 = (bf16[96,896]{1,0:T(8,128)(2,1)S(1)}, bf16[96,896]{1,0:T(8,128)(2,1)S(1)}, u32[]{:S(2)}, u32[]{:S(2)}) collective-permute-start(bf16[96,896]{1,0:T(8,128)(2,1)S(1)} %pad_maximum_fusion.2.x000), channel_id=1, source_target_pairs={{0,1},{1,0},{2,3},{3,2},{4,5},{5,4},{6,7},{7,6},{8,9},{9,8},{10,11... | collective-permute-start | bytes 516104 | tf_op jit(solution)/shard_map/ppermute | solution.py:305
  21.0 10.8 %collective-permute-start.8 = (bf16[96,896]{1,0:T(8,128)(2,1)S(1)}, bf16[96,896]{1,0:T(8,128)(2,1)S(1)}, u32[]{:S(2)}, u32[]{:S(2)}) collective-permute-start(bf16[96,896]{1,0:T(8,128)(2,1)S(1)} %pad_maximum_fusion.2.x000), channel_id=1, source_target_pairs={{0,5},{1,4},{2,7},{3,6},{4,1},{5,0},{6,3},{7,2},{8,13},{9,12},{10,... | collective-permute-start | bytes 516104 | tf_op jit(solution)/shard_map/ppermute | solution.py:306
  23.2 8.7 %collective-permute-start.15 = (bf16[96,896]{1,0:T(8,128)(2,1)}, bf16[96,896]{1,0:T(8,128)(2,1)S(1)}, u32[]{:S(2)}, u32[]{:S(2)}) collective-permute-start(bf16[96,896]{1,0:T(8,128)(2,1)} %slice.141), channel_id=1, source_target_pairs={{0,2},{2,0},{4,6},{6,4},{8,10},{10,8},{12,14},{14,12},{16,18},{18,... | collective-permute-start | bytes 516104 | tf_op jit(solution)/shard_map/ppermute | solution.py:303
  25.2 11.2 %collective-permute-start.16 = (bf16[96,896]{1,0:T(8,128)(2,1)S(1)}, bf16[96,896]{1,0:T(8,128)(2,1)S(1)}, u32[]{:S(2)}, u32[]{:S(2)}) collective-permute-start(bf16[96,896]{1,0:T(8,128)(2,1)S(1)} %slice.142), channel_id=1, source_target_pairs={{0,2},{2,0},{4,6},{6,4},{8,10},{10,8},{12,14},{14,12},{16,18},{18,... | collective-permute-start | bytes 516104 | tf_op jit(solution)/shard_map/ppermute | solution.py:303
  28.8 9.4 %collective-permute-start.5 = (bf16[96,896]{1,0:T(8,128)(2,1)S(1)}, bf16[96,896]{1,0:T(8,128)(2,1)S(1)}, u32[]{:S(2)}, u32[]{:S(2)}) collective-permute-start(bf16[96,896]{1,0:T(8,128)(2,1)S(1)} %pad_maximum_fusion.2.x000), channel_id=1, source_target_pairs={{0,2},{2,0},{4,6},{6,4},{8,10},{10,8},{12,14},{14,12},{16,18},{18,... | collective-permute-start | bytes 516104 | tf_op jit(solution)/shard_map/ppermute | solution.py:303
  28.8 9.4 %collective-permute-start.6 = (bf16[96,896]{1,0:T(8,128)(2,1)S(1)}, bf16[96,896]{1,0:T(8,128)(2,1)S(1)}, u32[]{:S(2)}, u32[]{:S(2)}) collective-permute-start(bf16[96,896]{1,0:T(8,128)(2,1)S(1)} %collective-permute-done.4.x001), channel_id=1, source_target_pairs={{0,2},{2,0},{4,6},{6,4},{8,10},{10,8},{12,14},{14,12},{16,18},{18,... | collective-permute-start | bytes 516104 | tf_op jit(solution)/shard_map/ppermute | solution.py:303
  31.8 6.5 %collective-permute-start.9 = (bf16[96,896]{1,0:T(8,128)(2,1)S(1)}, bf16[96,896]{1,0:T(8,128)(2,1)S(1)}, u32[]{:S(2)}, u32[]{:S(2)}) collective-permute-start(bf16[96,896]{1,0:T(8,128)(2,1)S(1)} %collective-permute-done.7.x100), channel_id=1, source_target_pairs={{0,2},{2,0},{4,6},{6,4},{8,10},{10,8},{12,14},{14,12},{16,18},{18,... | collective-permute-start | bytes 516104 | tf_op jit(solution)/shard_map/ppermute | solution.py:303
  31.8 6.5 %collective-permute-start.10 = (bf16[96,896]{1,0:T(8,128)(2,1)S(1)}, bf16[96,896]{1,0:T(8,128)(2,1)S(1)}, u32[]{:S(2)}, u32[]{:S(2)}) collective-permute-start(bf16[96,896]{1,0:T(8,128)(2,1)S(1)} %collective-permute-done.8.x101), channel_id=1, source_target_pairs={{0,2},{2,0},{4,6},{6,4},{8,10},{10,8},{12,14},{14,12},{16,18},{18,... | collective-permute-start | bytes 516104 | tf_op jit(solution)/shard_map/ppermute | solution.py:303
  37.7 4.8 %collective-permute-start.17 = (bf16[192,256]{1,0:T(8,128)(2,1)S(1)}, bf16[192,256]{1,0:T(8,128)(2,1)S(1)}, u32[]{:S(2)}, u32[]{:S(2)}) collective-permute-start(bf16[192,256]{1,0:T(8,128)(2,1)S(1)} %get-tuple-element.28), channel_id=1, source_target_pairs={{0,1},{1,0},{2,3},{3,2},{4,5},{5,4},{6,7},{7,6},{8,9},{9,8},{10,11... | collective-permute-start | bytes 294920 | tf_op jit(solution)/shard_map/ppermute | solution.py:305
  40.3 4.7 %collective-permute-start.12 = (bf16[192,256]{1,0:T(8,128)(2,1)S(1)}, bf16[192,256]{1,0:T(8,128)(2,1)S(1)}, u32[]{:S(2)}, u32[]{:S(2)}) collective-permute-start(bf16[192,256]{1,0:T(8,128)(2,1)S(1)} %get-tuple-element.23.own), channel_id=1, source_target_pairs={{0,1},{1,0},{2,3},{3,2},{4,5},{5,4},{6,7},{7,6},{8,9},{9,8},{10,11... | collective-permute-start | bytes 294920 | tf_op jit(solution)/shard_map/ppermute | solution.py:305
  44.0 5.4 %collective-permute-start.18 = (bf16[2,192,896]{2,1,0:T(8,128)(2,1)S(1)}, bf16[2,192,896]{2,1,0:T(8,128)(2,1)S(1)}, u32[]{:S(2)}, u32[]{:S(2)}) collective-permute-start(bf16[2,192,896]{2,1,0:T(8,128)(2,1)S(1)} %get-tuple-element.32), channel_id=1, source_target_pairs={{0,2},{2,0},{4,6},{6,4},{8,10},{10,8},{12,14},{14,12},{16,18},{18,... | collective-permute-start | bytes 2064392 | tf_op jit(solution)/shard_map/ppermute | solution.py:303
  46.1 1.7 %collective-permute-start.13 = (bf16[192,896]{1,0:T(8,128)(2,1)S(1)}, bf16[192,896]{1,0:T(8,128)(2,1)S(1)}, u32[]{:S(2)}, u32[]{:S(2)}) collective-permute-start(bf16[192,896]{1,0:T(8,128)(2,1)S(1)} %get-tuple-element.26), channel_id=1, source_target_pairs={{0,2},{2,0},{4,6},{6,4},{8,10},{10,8},{12,14},{14,12},{16,18},{18,... | collective-permute-start | bytes 1032200 | tf_op jit(solution)/shard_map/ppermute | solution.py:303
  47.9 7.3 %collective-permute-start.14 = (bf16[96,896]{1,0:T(8,128)(2,1)S(1)}, bf16[96,896]{1,0:T(8,128)(2,1)S(1)}, u32[]{:S(2)}, u32[]{:S(2)}) collective-permute-start(bf16[96,896]{1,0:T(8,128)(2,1)S(1)} %slice.186), channel_id=1, source_target_pairs={{0,4},{2,6},{4,0},{6,2},{8,12},{10,14},{12,8},{14,10},{16,20},{18,... | collective-permute-start | bytes 516104 | tf_op jit(solution)/shard_map/ppermute | solution.py:303
  49.7 10.2 %collective-permute-start.21 = (bf16[96,896]{1,0:T(8,128)(2,1)S(1)}, bf16[96,896]{1,0:T(8,128)(2,1)S(1)}, u32[]{:S(2)}, u32[]{:S(2)}) collective-permute-start(bf16[96,896]{1,0:T(8,128)(2,1)S(1)} %get-tuple-element.40), channel_id=1, source_target_pairs={{0,5},{1,4},{2,7},{3,6},{4,1},{5,0},{6,3},{7,2},{8,13},{9,12},{10,... | collective-permute-start | bytes 516104 | tf_op jit(solution)/shard_map/ppermute | solution.py:306
  51.2 9.5 %collective-permute-start.20 = (bf16[96,896]{1,0:T(8,128)(2,1)S(1)}, bf16[96,896]{1,0:T(8,128)(2,1)S(1)}, u32[]{:S(2)}, u32[]{:S(2)}) collective-permute-start(bf16[96,896]{1,0:T(8,128)(2,1)S(1)} %get-tuple-element.41), channel_id=1, source_target_pairs={{0,1},{1,0},{2,3},{3,2},{4,5},{5,4},{6,7},{7,6},{8,9},{9,8},{10,11... | collective-permute-start | bytes 516104 | tf_op jit(solution)/shard_map/ppermute | solution.py:305
  51.7 10.1 %collective-permute-start.19 = (bf16[96,896]{1,0:T(8,128)(2,1)S(1)}, bf16[96,896]{1,0:T(8,128)(2,1)S(1)}, u32[]{:S(2)}, u32[]{:S(2)}) collective-permute-start(bf16[96,896]{1,0:T(8,128)(2,1)S(1)} %get-tuple-element.39), channel_id=1, source_target_pairs={{0,4},{2,6},{4,0},{6,2},{8,12},{10,14},{12,8},{14,10},{16,20},{18,... | collective-permute-start | bytes 516104 | tf_op jit(solution)/shard_map/ppermute | solution.py:303
  62.0 10.5 %collective-permute-start.24 = (bf16[24,1792]{1,0:T(8,128)(2,1)S(1)}, bf16[24,1792]{1,0:T(8,128)(2,1)S(1)}, u32[]{:S(2)}, u32[]{:S(2)}) collective-permute-start(bf16[24,1792]{1,0:T(8,128)(2,1)S(1)} %get-tuple-element.43), channel_id=1, source_target_pairs={{0,8},{2,10},{4,12},{6,14},{8,0},{10,2},{12,4},{14,6},{16,24},{18,... | collective-permute-start | bytes 258056 | tf_op jit(solution)/shard_map/ppermute | solution.py:303
  62.7 9.8 %collective-permute-start.23 = (bf16[24,1792]{1,0:T(8,128)(2,1)S(1)}, bf16[24,1792]{1,0:T(8,128)(2,1)S(1)}, u32[]{:S(2)}, u32[]{:S(2)}) collective-permute-start(bf16[24,1792]{1,0:T(8,128)(2,1)S(1)} %get-tuple-element.44), channel_id=1, source_target_pairs={{0,16},{2,18},{4,20},{6,22},{8,24},{10,26},{12,28},{14,30},{16,0},... | collective-permute-start | bytes 258056 | tf_op jit(solution)/shard_map/ppermute | solution.py:303
  65.1 7.4 %collective-permute-start.22 = (bf16[24,1792]{1,0:T(8,128)(2,1)S(1)}, bf16[24,1792]{1,0:T(8,128)(2,1)S(1)}, u32[]{:S(2)}, u32[]{:S(2)}) collective-permute-start(bf16[24,1792]{1,0:T(8,128)(2,1)S(1)} %get-tuple-element.42), channel_id=1, source_target_pairs={{0,24},{2,26},{4,28},{6,30},{8,16},{10,18},{12,20},{14,22},{16,8},... | collective-permute-start | bytes 258056 | tf_op jit(solution)/shard_map/ppermute | solution.py:303
  (5 other events, 37.5 us)
where the time goes:
time: 74.8 us; the launch traced here: 74.5 us
  waiting for transfers between devices  29.2 us (39%)
  starting transfers between devices  24.3 us (32%)
  Pallas kernels  13 us (17%)
  local copies, waits for them, and re-layouts  4.02 us (5%)
  other arithmetic  3.09 us (4%)
  between operations  0.92 us (1%)
    ppermute x20, waiting for transfers between devices, swap(): lax.ppermute(value, 'expert', [(i, i ^ expert_bits) for i in range(count)])  19.8 us
    ppermute x20, starting transfers between devices, swap(): lax.ppermute(value, 'expert', [(i, i ^ expert_bits) for i in range(count)])  17.2 us
    pallas_call x7, Pallas kernels, call(): pl.pallas_call(kernel, out_shape=list(outs), in_specs=[pl.BlockSpec(memor...  13 us
    ppermute x2, waiting for transfers between devices, swap(): lax.ppermute(value, ('expert', 'replica'), [(i, i ^ flip) for i in range(...  7.12 us
    ppermute x4, starting transfers between devices, swap(): lax.ppermute(value, 'replica', [(i, i ^ flip) for i in range(replicas)])  4.18 us
    unnamed x6, local copies, waits for them, and re-layouts  3 us
    ppermute x2, starting transfers between devices, swap(): lax.ppermute(value, ('expert', 'replica'), [(i, i ^ flip) for i in range(...  2.99 us
    ppermute x4, waiting for transfers between devices, swap(): lax.ppermute(value, 'replica', [(i, i ^ flip) for i in range(replicas)])  2.33 us
  transfers between devices with their start and end apart: 26, of which 14 were waited for; matrix products, arithmetic and copies ran while one was open for 2% of the time, Pallas kernels for 17%

commit v1 on v0

--- a/solution.py
+++ b/solution.py
@@ -182,6 +182,10 @@
     return pl.ds(pl.multiple_of(index * width, width), width)
 
 
+def quarter(place, r_rel, c_rel, width):
+    return columns((place[0] ^ r_rel) * 2 + (place[1] ^ c_rel), width)
+
+
 def load_kernel(place, gate_hbm, up_hbm, down_hbm, gate, up, down, sems):
     copies = [pltpu.make_async_copy(source, target, sems.at[n])
               for n, (source, target) in enumerate(
@@ -205,18 +209,26 @@
     give[...] = total[1].astype(give.dtype)
 
 
-def hidden_kernel(place, x000, x001, x010, x011, x100, x101, x110, x111, t0, t1, gate, up,
-                  hidden, act, slope):
-    width = x000.shape[1]
+def products(place, c_rel, x, gate, up):
+    width = x[0].shape[1]
     a = b = None
-    for r_rel, c_rel, parts in ((0, 0, (x000, x001)), (0, 1, (x010, x011)),
-                                (1, 0, (x100, x101)), (1, 1, (x110, x111))):
-        rows = jnp.concatenate([part[...] for part in parts], axis=0)
-        where = columns((place[0] ^ r_rel) * 2 + (place[1] ^ c_rel), width)
+    for r_rel in range(2):
+        rows = jnp.concatenate([part[...] for part in x[2 * r_rel : 2 * r_rel + 2]], axis=0)
+        where = quarter(place, r_rel, c_rel, width)
         term_a = dot(rows, gate[:, where], ((1,), (1,)))
         term_b = dot(rows, up[:, where], ((1,), (1,)))
         a = term_a if a is None else a + term_a
         b = term_b if b is None else b + term_b
+    return a, b
+
+
+def half_kernel(place, x00, x01, x10, x11, gate, up, a_out, b_out):
+    a_out[...], b_out[...] = products(place, 0, (x00, x01, x10, x11), gate, up)
+
+
+def hidden_kernel(place, a_in, b_in, x00, x01, x10, x11, t0, t1, gate, up, hidden, act, slope):
+    a, b = products(place, 1, (x00, x01, x10, x11), gate, up)
+    a, b = a + a_in[...], b + b_in[...]
     weight = gate_column(place, (t0, t1))
     sigma = jax.nn.sigmoid(a)
     silu = a * sigma
@@ -225,21 +237,26 @@
     slope[...] = weight * (b * (sigma * (1.0 + a * (1.0 - sigma))))
 
 
-def input_kernel(place, own, other, act, slope, gate, up, da_out, db_out, keep, give):
-    width = keep.shape[2]
+def give_kernel(place, own, other, act, slope, gate, up, da_out, db_out, give):
+    width = give.shape[2]
     dh = own[...] + other[...].astype(F32)
     da = (dh * slope[...]).astype(BF16)
     db = (dh * act[...]).astype(BF16)
     da_out[...] = da
     db_out[...] = db
     for r_rel in range(2):
-        for c_rel in range(2):
-            where = columns((place[0] ^ r_rel) * 2 + (place[1] ^ c_rel), width)
-            block = dot(da, gate[:, where], ((1,), (0,))) + dot(db, up[:, where], ((1,), (0,)))
-            if c_rel == 0:
-                keep[r_rel] = block
-            else:
-                give[r_rel] = block.astype(give.dtype)
+        where = quarter(place, r_rel, 1, width)
+        block = dot(da, gate[:, where], ((1,), (0,))) + dot(db, up[:, where], ((1,), (0,)))
+        give[r_rel] = block.astype(give.dtype)
+
+
+def keep_kernel(place, da, db, gate, up, keep):
+    width = keep.shape[2]
+    for r_rel in range(2):
+        where = quarter(place, r_rel, 0, width)
+        keep[r_rel] = dot(da[...], gate[:, where], ((1,), (0,))) + dot(
+            db[...], up[:, where], ((1,), (0,))
+        )
 
 
 def output_kernel(place, own, other, down, keep, give):
@@ -254,29 +271,40 @@
             give[...] = block.astype(give.dtype)
 
 
-def down_grad_kernel(place, own, other, og00, og01, og10, og11, down_grad):
+def down_grad_kernel(place, own, other, og00, og01, og10, og11, down_grad, made, sems):
     width, units = og10.shape[1], own.shape[1]
+    copies = []
     for c_rel, parts in enumerate(((og00, og01), (og10, og11))):
         rows = jnp.concatenate([part[:, :width] for part in parts], axis=0)
         for r_rel, hidden in ((0, own), (1, other)):
-            block = dot(hidden[...], rows, ((0,), (0,)))
-            down_grad[columns(place[0] ^ r_rel, units), columns(place[1] ^ c_rel, width)] = (
-                block.astype(down_grad.dtype)
-            )
+            n = len(copies)
+            made[n] = dot(hidden[...], rows, ((0,), (0,))).astype(made.dtype)
+            where = columns(place[0] ^ r_rel, units), columns(place[1] ^ c_rel, width)
+            copies.append(pltpu.make_async_copy(made.at[n], down_grad.at[where], sems.at[n]))
+            copies[n].start()
+    for copy in copies:
+        copy.wait()
 
 
 def weight_grad_kernel(place, da, db, x000, x001, x010, x011, x100, x101, x110, x111,
-                       gate_grad, up_grad):
+                       gate_grad, up_grad, made, sems):
     width = x000.shape[1]
+    copies = []
     for r_rel, c_rel, parts in ((0, 0, (x000, x001)), (0, 1, (x010, x011)),
                                 (1, 0, (x100, x101)), (1, 1, (x110, x111))):
         rows = jnp.concatenate([part[...] for part in parts], axis=0)
-        where = columns((place[0] ^ r_rel) * 2 + (place[1] ^ c_rel), width)
-        gate_grad[:, where] = dot(da[...], rows, ((0,), (0,))).astype(gate_grad.dtype)
-        up_grad[:, where] = dot(db[...], rows, ((0,), (0,))).astype(up_grad.dtype)
-
-
-def call(kernel, place, operands, outs, flops, in_hbm=(), scratch=(), limit=24 << 20):
+        where = slice(None), quarter(place, r_rel, c_rel, width)
+        for source, target in ((da, gate_grad), (db, up_grad)):
+            n = len(copies)
+            made[n] = dot(source[...], rows, ((0,), (0,))).astype(made.dtype)
+            copies.append(pltpu.make_async_copy(made.at[n], target.at[where], sems.at[n]))
+            copies[n].start()
+    for copy in copies:
+        copy.wait()
+
+
+def call(kernel, place, operands, outs, flops, in_hbm=(), scratch=(), limit=24 << 20,
+         out_hbm=False):
     moved = sum(x.size * x.dtype.itemsize for x in (*operands, *outs))
     vmem = pl.BlockSpec(memory_space=pltpu.VMEM)
     hbm = pl.BlockSpec(memory_space=pltpu.HBM)
@@ -285,7 +313,7 @@
         out_shape=list(outs),
         in_specs=[pl.BlockSpec(memory_space=pltpu.SMEM)]
         + [hbm if n in in_hbm else vmem for n in range(len(operands))],
-        out_specs=[vmem] * len(outs),
+        out_specs=[hbm if out_hbm else vmem] * len(outs),
         scratch_shapes=list(scratch),
         compiler_params=pltpu.CompilerParams(vmem_limit_bytes=limit),
         cost_estimate=pl.CostEstimate(flops=flops, bytes_accessed=moved, transcendentals=0),
@@ -366,20 +394,29 @@
         work * 2 * slice_width,
     )
     d_got = swap(d_give, 0, 1)
+    of_units = struct((all_rows, units), F32)
+    of_units_low = struct((all_rows, units), BF16)
+    straight, crossed = (x[0], x[1], x[4], x[5]), (x[2], x[3], x[6], x[7])
+    a_half, b_half = call(
+        half_kernel, place, (*straight, gate, up), (of_units, of_units),
+        work * model_width,
+    )
     hidden, act, slope = call(
-        hidden_kernel, place, (*x, og_here, og_side, gate, up),
-        (struct((all_rows, units), BF16), struct((all_rows, units), F32),
-         struct((all_rows, units), F32)),
-        work * 2 * model_width,
+        hidden_kernel, place,
+        (a_half, b_half, *crossed, og_here, og_side, gate, up),
+        (of_units_low, of_units, of_units), work * model_width,
     )
     hidden_got = swap(hidden, 0, 1)
-    da, db, dx_keep, dx_give = call(
-        input_kernel, place, (d_own, d_got, act, slope, gate, up),
-        (struct((all_rows, units), BF16), struct((all_rows, units), BF16),
-         struct((2, all_rows, half), F32), struct((2, all_rows, half), BF16)),
-        work * 2 * model_width,
-    )
-    dx = dx_keep + swap(dx_give, 1).astype(F32)
+    da, db, dx_give = call(
+        give_kernel, place, (d_own, d_got, act, slope, gate, up),
+        (of_units_low, of_units_low, struct((2, all_rows, half), BF16)), work * model_width,
+    )
+    dx_got = swap(dx_give, 1)
+    (dx_keep,) = call(
+        keep_kernel, place, (da, db, gate, up),
+        (struct((2, all_rows, half), F32),), work * model_width,
+    )
+    dx = dx_keep + dx_got.astype(F32)
     dx_cross = swap(dx[1, side_rows:].astype(BF16), 2, 1)
     dx_side = swap(dx[0, side_rows:].astype(BF16), 2)
     dx_up = swap(dx[1, :side_rows].astype(BF16), 0, 1)
@@ -390,25 +427,35 @@
         work * 2 * slice_width,
     )
     y = y_keep + swap(y_give, 1).astype(F32)
-    y_side = swap(y[side_rows:].astype(BF16), 2)
     (down_grad,) = call(
         down_grad_kernel, place, (hidden, hidden_got, *og),
-        (struct(down.shape, BF16),), work * 2 * slice_width,
+        (struct(down.shape, BF16),), work * 2 * slice_width, out_hbm=True,
+        scratch=[pltpu.VMEM((4, units, half), BF16), pltpu.SemaphoreType.DMA((4,))],
     )
     gate_grad, up_grad = call(
         weight_grad_kernel, place, (da, db, *x),
-        (struct(gate.shape, BF16), struct(up.shape, BF16)), work * 2 * model_width,
-    )
-
-    dx_sum = (dx[0, :side_rows] + dx_side.astype(F32)) + (dx_up.astype(F32) + dx_cross.astype(F32))
-    y_sum = y[:side_rows] + y_side.astype(F32)
-    both = jnp.concatenate([y_sum, dx_sum], axis=1)
+        (struct(gate.shape, BF16), struct(up.shape, BF16)), work * 2 * model_width, out_hbm=True,
+        scratch=[pltpu.VMEM((8, units, half), BF16), pltpu.SemaphoreType.DMA((8,))],
+    )
+
     pair = 2 * tok_rows
-    total = both[:pair]
-    for step in reversed(range(1, far)):
-        part = both[step * pair : (step + 1) * pair].astype(BF16)
-        total = total + swap(part, 4 * step).astype(F32)
-    total = total.astype(BF16)
+
+    def far_sum(parts):
+        got = [swap(parts[step].astype(BF16), 4 * step) for step in reversed(range(1, far))]
+        return sum((value.astype(F32) for value in got), parts[0])
+
+    def rows_of(value, step):
+        return value[step * pair : (step + 1) * pair]
+
+    y_pair = far_sum([
+        jnp.concatenate([rows_of(y, step), rows_of(y, far + step)], axis=0) for step in range(far)
+    ])
+    y_sum = y_pair[:pair] + swap(y_pair[pair:].astype(BF16), 2).astype(F32)
+    dx_near = (dx[0, :side_rows] + dx_side.astype(F32)) + (
+        dx_up.astype(F32) + dx_cross.astype(F32)
+    )
+    dx_sum = far_sum([rows_of(dx_near, step) for step in range(far)])
+    total = jnp.concatenate([y_sum, dx_sum], axis=1).astype(BF16)
     first, second = total[:tok_rows], total[tok_rows:]
     kept = jnp.where(core == 0, first, second)
     got = swap(jnp.where(core == 0, second, first), 1)

time: 74.8 us -> 81.9 us (1.095)
  waiting for transfers between devices: 29.2 us -> 34.6 us
  starting transfers between devices: 24.3 us -> 25.5 us
  Pallas kernels: 13 us -> 14 us
    ppermute x4, waiting for transfers between devices: 2.33 us -> 11.9 us  [swap(): lax.ppermute(value, 'replica', [(i, i ^ flip) for i in range(replicas)])]
    ppermute x20 -> x23, starting transfers between devices: 17.2 us -> 21.2 us  [swap(): lax.ppermute(value, 'expert', [(i, i ^ expert_bits) for i in range(count)])]
    ppermute x4, starting transfers between devices: 4.18 us -> 1.49 us  [swap(): lax.ppermute(value, 'replica', [(i, i ^ flip) for i in range(replicas)])]
    ppermute x20 -> x23, waiting for transfers between devices: 19.8 us -> 17.5 us  [swap(): lax.ppermute(value, 'expert', [(i, i ^ expert_bits) for i in range(count)])]
    ppermute x2, waiting for transfers between devices: 7.12 us -> 5.2 us  [swap(): lax.ppermute(value, ('expert', 'replica'), [(i, i ^ flip) for i in range(...]
    pallas_call x7 -> x9, Pallas kernels: 13 us -> 14 us  [call(): pl.pallas_call(kernel, out_shape=list(outs), in_specs=[pl.BlockSpec(memor...]
  transfers between devices with their start and end apart: 26 -> 29, of which waited for: 14 -> 17; matrix products, arithmetic and copies ran while one was open for 2% -> 1% of each run, Pallas kernels for 17% -> 15%
where the time goes in v1:
time: 81.9 us; the launch traced here: 81.6 us
  waiting for transfers between devices  34.6 us (42%)
  starting transfers between devices  25.5 us (31%)
  Pallas kernels  14 us (17%)
  local copies, waits for them, and re-layouts  3.36 us (4%)
  other arithmetic  3.12 us (4%)
  between operations  1.02 us (1%)
    ppermute x23, starting transfers between devices, swap(): lax.ppermute(value, 'expert', [(i, i ^ expert_bits) for i in range(count)])  21.2 us
    ppermute x23, waiting for transfers between devices, swap(): lax.ppermute(value, 'expert', [(i, i ^ expert_bits) for i in range(count)])  17.5 us
    pallas_call x9, Pallas kernels, call(): pl.pallas_call(kernel, out_shape=list(outs), in_specs=[pl.BlockSpec(memor...  14 us
    ppermute x4, waiting for transfers between devices, swap(): lax.ppermute(value, 'replica', [(i, i ^ flip) for i in range(replicas)])  11.9 us
    ppermute x2, waiting for transfers between devices, swap(): lax.ppermute(value, ('expert', 'replica'), [(i, i ^ flip) for i in range(...  5.2 us
    unnamed x6, local copies, waits for them, and re-layouts  3.01 us
    ppermute x2, starting transfers between devices, swap(): lax.ppermute(value, ('expert', 'replica'), [(i, i ^ flip) for i in range(...  2.82 us
  transfers between devices with their start and end apart: 29, of which 17 were waited for; matrix products, arithmetic and copies ran while one was open for 1% of the time, Pallas kernels for 15%

profile of v1, /device:TPU:0, one launch (start us, length us, event | category | flops | bytes accessed | tf_op | source)
XLA Modules:
  0.0 81.6 jit_solution(12179171140087241089)
XLA Ops:
  4.2 5.0 %collective-permute-start.3 = (bf16[24,1920]{1,0:T(8,128)(2,1)S(1)}, bf16[24,1920]{1,0:T(8,128)(2,1)S(1)}, u32[]{:S(2)}, u32[]{:S(2)}) collective-permute-start(bf16[24,1920]{1,0:T(8,128)(2,1)S(1)} %maximum_select_fusion), channel_id=1, source_target_pairs={{0,24},{2,26},{4,28},{6,30},{8,16},{10,18},{12,20},{14,22},{16,8},... | collective-permute-start | bytes 276488 | tf_op jit(solution)/shard_map/ppermute | solution.py:331
  9.9 3.0 %collective-permute-done.3 = bf16[24,1920]{1,0:T(8,128)(2,1)S(1)} collective-permute-done((bf16[24,1920]{1,0:T(8,128)(2,1)S(1)}, bf16[24,1920]{1,0:T(8,128)(2,1)S(1)}, u32[]{:S(2)}, u32[]{:S(2)}) %collective-permute-start.3) | collective-permute-done | bytes 92192 | tf_op jit(solution)/shard_map/ppermute | solution.py:331
  12.8 4.4 %collective-permute-done.2 = bf16[24,1920]{1,0:T(8,128)(2,1)S(1)} collective-permute-done((bf16[24,1920]{1,0:T(8,128)(2,1)S(1)}, bf16[24,1920]{1,0:T(8,128)(2,1)S(1)}, u32[]{:S(2)}, u32[]{:S(2)}) %collective-permute-start.2) | collective-permute-done | bytes 92192 | tf_op jit(solution)/shard_map/ppermute | solution.py:331
  17.3 2.5 %collective-permute-start.6 = (bf16[96,896]{1,0:T(8,128)(2,1)S(1)}, bf16[96,896]{1,0:T(8,128)(2,1)S(1)}, u32[]{:S(2)}, u32[]{:S(2)}) collective-permute-start(bf16[96,896]{1,0:T(8,128)(2,1)S(1)} %pad_maximum_fusion.1.x00.x000), channel_id=1, source_target_pairs={{0,5},{1,4},{2,7},{3,6},{4,1},{5,0},{6,3},{7,2},{8,13},{9,12},{10,... | collective-permute-start | bytes 516104 | tf_op jit(solution)/shard_map/ppermute | solution.py:334
  20.9 1.6 %collective-permute-start.11 = (bf16[96,1024]{1,0:T(8,128)(2,1)S(1)}, bf16[96,1024]{1,0:T(8,128)(2,1)S(1)}, u32[]{:S(2)}, u32[]{:S(2)}) collective-permute-start(bf16[96,1024]{1,0:T(8,128)(2,1)S(1)} %pad_maximum_fusion.t0.og00), channel_id=1, source_target_pairs={{0,4},{2,6},{4,0},{6,2},{8,12},{10,14},{12,8},{14,10},{16,20},{18,... | collective-permute-start | bytes 589832 | tf_op jit(solution)/shard_map/ppermute | solution.py:331
  22.5 2.6 %collective-permute-done.6.x11.x101 = bf16[96,896]{1,0:T(8,128)(2,1)S(1)} collective-permute-done((bf16[96,896]{1,0:T(8,128)(2,1)S(1)}, bf16[96,896]{1,0:T(8,128)(2,1)S(1)}, u32[]{:S(2)}, u32[]{:S(2)}) %collective-permute-start.6) | collective-permute-done | bytes 172064 | tf_op jit(solution)/shard_map/ppermute | solution.py:334
  25.1 2.4 %collective-permute-done.5.x10.x100 = bf16[96,896]{1,0:T(8,128)(2,1)S(1)} collective-permute-done((bf16[96,896]{1,0:T(8,128)(2,1)S(1)}, bf16[96,896]{1,0:T(8,128)(2,1)S(1)}, u32[]{:S(2)}, u32[]{:S(2)}) %collective-permute-start.5) | collective-permute-done | bytes 172064 | tf_op jit(solution)/shard_map/ppermute | solution.py:333
  27.6 1.7 %collective-permute-done.4.x01.x001 = bf16[96,896]{1,0:T(8,128)(2,1)S(1)} collective-permute-done((bf16[96,896]{1,0:T(8,128)(2,1)S(1)}, bf16[96,896]{1,0:T(8,128)(2,1)S(1)}, u32[]{:S(2)}, u32[]{:S(2)}) %collective-permute-start.4) | collective-permute-done | bytes 172064 | tf_op jit(solution)/shard_map/ppermute | solution.py:331
  29.4 1.5 %copy-done.1 = bf16[1,256,3584]{2,1,0:T(8,128)(2,1)S(1)} copy-done((bf16[1,256,3584]{2,1,0:T(8,128)(2,1)S(1)}, bf16[1,256,3584]{2,1,0:T(8,128)(2,1)}, u32[]{:S(2)}) %copy-start.1) | copy-done | bytes 1835032
  30.9 1.5 %copy-done.2 = bf16[1,512,1792]{2,1,0:T(8,128)(2,1)S(1)} copy-done((bf16[1,512,1792]{2,1,0:T(8,128)(2,1)S(1)}, bf16[1,512,1792]{2,1,0:T(8,128)(2,1)}, u32[]{:S(2)}) %copy-start.2) | copy-done | bytes 1835032
  34.7 1.8 %shard_map.112 = (bf16[192,256]{1,0:T(8,128)(2,1)S(1)}, f32[192,256]{1,0:T(8,128)S(1)}, f32[192,256]{1,0:T(8,128)S(1)}) custom-call(s32[4]{0:T(128)S(1)} %pad_add_fusion.place, f32[192,256]{1,0:T(8,128)S(1)} %get-tuple-element.24.a_in, f32[192,256]{1,0:T(8,128)S(1)} %get-tuple-element.25.b_in, bf16[96,896]{1,0:T(8,128)(2,1)S(1)} %collective-permute-done.7.x00.x010, ...), custom_call_target="tpu_custom_call" | custom-call | flops 352321536 | bytes 5636096 | tf_op jit(solution)/shard_map/pallas_call | solution.py:311
  37.5 4.3 %collective-permute-done.12.other = bf16[192,256]{1,0:T(8,128)(2,1)S(1)} collective-permute-done((bf16[192,256]{1,0:T(8,128)(2,1)S(1)}, bf16[192,256]{1,0:T(8,128)(2,1)S(1)}, u32[]{:S(2)}, u32[]{:S(2)}) %collective-permute-start.12) | collective-permute-done | bytes 98336 | tf_op jit(solution)/shard_map/ppermute | solution.py:333
  44.7 2.1 %shard_map.118 = bf16[512,1792]{1,0:T(8,128)(2,1)} custom-call(s32[4]{0:T(128)S(1)} %pad_add_fusion.place, bf16[192,256]{1,0:T(8,128)(2,1)S(1)} %get-tuple-element.26.own, bf16[192,256]{1,0:T(8,128)(2,1)S(1)} %collective-permute-done.12.other, bf16[96,1024]{1,0:T(8,128)(2,1)S(1)} %pad_maximum_fusion.t0.og00, ...), custom_call_target="tpu_custom_call" | custom-call | flops 352321536 | bytes 2768896 | tf_op jit(solution)/shard_map/pallas_call | solution.py:311
  46.8 2.8 %collective-permute-done.20.other = bf16[192,256]{1,0:T(8,128)(2,1)S(1)} collective-permute-done((bf16[192,256]{1,0:T(8,128)(2,1)S(1)}, bf16[192,256]{1,0:T(8,128)(2,1)S(1)}, u32[]{:S(2)}, u32[]{:S(2)}) %collective-permute-start.20) | collective-permute-done | bytes 98336 | tf_op jit(solution)/shard_map/ppermute | solution.py:333
  51.9 3.1 %shard_map.117 = (bf16[256,3584]{1,0:T(8,128)(2,1)}, bf16[256,3584]{1,0:T(8,128)(2,1)}) custom-call(s32[4]{0:T(128)S(1)} %pad_add_fusion.place, bf16[192,256]{1,0:T(8,128)(2,1)S(1)} %get-tuple-element.34.da, bf16[192,256]{1,0:T(8,128)(2,1)S(1)} %get-tuple-element.35.db, bf16[96,896]{1,0:T(8,128)(2,1)S(1)} %pad_maximum_fusion.1.x00.x000, ...), custom_call_target="tpu_custom_call" | custom-call | flops 704643072 | bytes 5242880 | tf_op jit(solution)/shard_map/pallas_call | solution.py:311
  55.3 3.1 %collective-permute-start.16 = (bf16[48,896]{1,0:T(8,128)(2,1)S(1)}, bf16[48,896]{1,0:T(8,128)(2,1)S(1)}, u32[]{:S(2)}, u32[]{:S(2)}) collective-permute-start(bf16[48,896]{1,0:T(8,128)(2,1)S(1)} %pad_maximum_fusion.5), channel_id=1, source_target_pairs={{0,8},{2,10},{4,12},{6,14},{8,0},{10,2},{12,4},{14,6},{16,24},{18,... | collective-permute-start | bytes 258056 | tf_op jit(solution)/shard_map/ppermute | solution.py:331
  60.1 1.5 %collective-permute-start.22 = (bf16[96,896]{1,0:T(8,128)(2,1)S(1)}, bf16[96,896]{1,0:T(8,128)(2,1)S(1)}, u32[]{:S(2)}, u32[]{:S(2)}) collective-permute-start(bf16[96,896]{1,0:T(8,128)(2,1)S(1)} %get-tuple-element.47), channel_id=1, source_target_pairs={{0,4},{2,6},{4,0},{6,2},{8,12},{10,14},{12,8},{14,10},{16,20},{18,... | collective-permute-start | bytes 516104 | tf_op jit(solution)/shard_map/ppermute | solution.py:331
  61.9 1.5 %collective-permute-done.15 = bf16[48,896]{1,0:T(8,128)(2,1)S(1)} collective-permute-done((bf16[48,896]{1,0:T(8,128)(2,1)S(1)}, bf16[48,896]{1,0:T(8,128)(2,1)S(1)}, u32[]{:S(2)}, u32[]{:S(2)}) %collective-permute-start.15) | collective-permute-done | bytes 86048 | tf_op jit(solution)/shard_map/ppermute | solution.py:331
  65.1 1.5 %collective-permute-start.17 = (bf16[24,896]{1,0:T(8,128)(2,1)S(1)}, bf16[24,896]{1,0:T(8,128)(2,1)S(1)}, u32[]{:S(2)}, u32[]{:S(2)}) collective-permute-start(bf16[24,896]{1,0:T(8,128)(2,1)S(1)} %slice.236), channel_id=1, source_target_pairs={{0,4},{2,6},{4,0},{6,2},{8,12},{10,14},{12,8},{14,10},{16,20},{18,... | collective-permute-start | bytes 129032 | tf_op jit(solution)/shard_map/ppermute | solution.py:331
  67.4 2.6 %collective-permute-done.24 = bf16[96,896]{1,0:T(8,128)(2,1)S(1)} collective-permute-done((bf16[96,896]{1,0:T(8,128)(2,1)S(1)}, bf16[96,896]{1,0:T(8,128)(2,1)S(1)}, u32[]{:S(2)}, u32[]{:S(2)}) %collective-permute-start.24) | collective-permute-done | bytes 172064 | tf_op jit(solution)/shard_map/ppermute | solution.py:334
  70.0 2.4 %collective-permute-done.23 = bf16[96,896]{1,0:T(8,128)(2,1)S(1)} collective-permute-done((bf16[96,896]{1,0:T(8,128)(2,1)S(1)}, bf16[96,896]{1,0:T(8,128)(2,1)S(1)}, u32[]{:S(2)}, u32[]{:S(2)}) %collective-permute-start.23) | collective-permute-done | bytes 172064 | tf_op jit(solution)/shard_map/ppermute | solution.py:333
  72.5 1.9 %collective-permute-start.25 = (bf16[24,896]{1,0:T(8,128)(2,1)S(1)}, bf16[24,896]{1,0:T(8,128)(2,1)S(1)}, u32[]{:S(2)}, u32[]{:S(2)}) collective-permute-start(bf16[24,896]{1,0:T(8,128)(2,1)S(1)} %get-tuple-element.56), channel_id=1, source_target_pairs={{0,24},{2,26},{4,28},{6,30},{8,16},{10,18},{12,20},{14,22},{16,8},... | collective-permute-start | bytes 129032 | tf_op jit(solution)/shard_map/ppermute | solution.py:331
  74.4 2.5 %collective-permute-start.26 = (bf16[24,896]{1,0:T(8,128)(2,1)S(1)}, bf16[24,896]{1,0:T(8,128)(2,1)S(1)}, u32[]{:S(2)}, u32[]{:S(2)}) collective-permute-start(bf16[24,896]{1,0:T(8,128)(2,1)S(1)} %get-tuple-element.58), channel_id=1, source_target_pairs={{0,16},{2,18},{4,20},{6,22},{8,24},{10,26},{12,28},{14,30},{16,0},... | collective-permute-start | bytes 129032 | tf_op jit(solution)/shard_map/ppermute | solution.py:331
  77.0 1.4 %collective-permute-done.25 = bf16[24,896]{1,0:T(8,128)(2,1)S(1)} collective-permute-done((bf16[24,896]{1,0:T(8,128)(2,1)S(1)}, bf16[24,896]{1,0:T(8,128)(2,1)S(1)}, u32[]{:S(2)}, u32[]{:S(2)}) %collective-permute-start.25) | collective-permute-done | bytes 43040 | tf_op jit(solution)/shard_map/ppermute | solution.py:331
  (90 shorter events, 21.7 us)
Async XLA Ops:
  4.2 8.6 %collective-permute-start.3 = (bf16[24,1920]{1,0:T(8,128)(2,1)S(1)}, bf16[24,1920]{1,0:T(8,128)(2,1)S(1)}, u32[]{:S(2)}, u32[]{:S(2)}) collective-permute-start(bf16[24,1920]{1,0:T(8,128)(2,1)S(1)} %maximum_select_fusion), channel_id=1, source_target_pairs={{0,24},{2,26},{4,28},{6,30},{8,16},{10,18},{12,20},{14,22},{16,8},... | collective-permute-start | bytes 276488 | tf_op jit(solution)/shard_map/ppermute | solution.py:331
  9.2 8.1 %collective-permute-start.2 = (bf16[24,1920]{1,0:T(8,128)(2,1)S(1)}, bf16[24,1920]{1,0:T(8,128)(2,1)S(1)}, u32[]{:S(2)}, u32[]{:S(2)}) collective-permute-start(bf16[24,1920]{1,0:T(8,128)(2,1)S(1)} %maximum_select_fusion), channel_id=1, source_target_pairs={{0,16},{2,18},{4,20},{6,22},{8,24},{10,26},{12,28},{14,30},{16,0},... | collective-permute-start | bytes 276488 | tf_op jit(solution)/shard_map/ppermute | solution.py:331
  9.2 8.1 %collective-permute-start.1 = (bf16[24,1920]{1,0:T(8,128)(2,1)S(1)}, bf16[24,1920]{1,0:T(8,128)(2,1)S(1)}, u32[]{:S(2)}, u32[]{:S(2)}) collective-permute-start(bf16[24,1920]{1,0:T(8,128)(2,1)S(1)} %maximum_select_fusion), channel_id=1, source_target_pairs={{0,8},{2,10},{4,12},{6,14},{8,0},{10,2},{12,4},{14,6},{16,24},{18,... | collective-permute-start | bytes 276488 | tf_op jit(solution)/shard_map/ppermute | solution.py:331
  17.3 7.8 %collective-permute-start.6 = (bf16[96,896]{1,0:T(8,128)(2,1)S(1)}, bf16[96,896]{1,0:T(8,128)(2,1)S(1)}, u32[]{:S(2)}, u32[]{:S(2)}) collective-permute-start(bf16[96,896]{1,0:T(8,128)(2,1)S(1)} %pad_maximum_fusion.1.x00.x000), channel_id=1, source_target_pairs={{0,5},{1,4},{2,7},{3,6},{4,1},{5,0},{6,3},{7,2},{8,13},{9,12},{10,... | collective-permute-start | bytes 516104 | tf_op jit(solution)/shard_map/ppermute | solution.py:334
  19.8 7.7 %collective-permute-start.5 = (bf16[96,896]{1,0:T(8,128)(2,1)S(1)}, bf16[96,896]{1,0:T(8,128)(2,1)S(1)}, u32[]{:S(2)}, u32[]{:S(2)}) collective-permute-start(bf16[96,896]{1,0:T(8,128)(2,1)S(1)} %pad_maximum_fusion.1.x00.x000), channel_id=1, source_target_pairs={{0,1},{1,0},{2,3},{3,2},{4,5},{5,4},{6,7},{7,6},{8,9},{9,8},{10,11... | collective-permute-start | bytes 516104 | tf_op jit(solution)/shard_map/ppermute | solution.py:333
  20.3 9.0 %collective-permute-start.4 = (bf16[96,896]{1,0:T(8,128)(2,1)S(1)}, bf16[96,896]{1,0:T(8,128)(2,1)S(1)}, u32[]{:S(2)}, u32[]{:S(2)}) collective-permute-start(bf16[96,896]{1,0:T(8,128)(2,1)S(1)} %pad_maximum_fusion.1.x00.x000), channel_id=1, source_target_pairs={{0,4},{2,6},{4,0},{6,2},{8,12},{10,14},{12,8},{14,10},{16,20},{18,... | collective-permute-start | bytes 516104 | tf_op jit(solution)/shard_map/ppermute | solution.py:331
  20.9 13.7 %collective-permute-start.11 = (bf16[96,1024]{1,0:T(8,128)(2,1)S(1)}, bf16[96,1024]{1,0:T(8,128)(2,1)S(1)}, u32[]{:S(2)}, u32[]{:S(2)}) collective-permute-start(bf16[96,1024]{1,0:T(8,128)(2,1)S(1)} %pad_maximum_fusion.t0.og00), channel_id=1, source_target_pairs={{0,4},{2,6},{4,0},{6,2},{8,12},{10,14},{12,8},{14,10},{16,20},{18,... | collective-permute-start | bytes 589832 | tf_op jit(solution)/shard_map/ppermute | solution.py:331
  22.5 12.2 %collective-permute-start.7 = (bf16[96,896]{1,0:T(8,128)(2,1)S(1)}, bf16[96,896]{1,0:T(8,128)(2,1)S(1)}, u32[]{:S(2)}, u32[]{:S(2)}) collective-permute-start(bf16[96,896]{1,0:T(8,128)(2,1)S(1)} %pad_maximum_fusion.1.x00.x000), channel_id=1, source_target_pairs={{0,2},{2,0},{4,6},{6,4},{8,10},{10,8},{12,14},{14,12},{16,18},{18,... | collective-permute-start | bytes 516104 | tf_op jit(solution)/shard_map/ppermute | solution.py:331
  25.1 9.6 %collective-permute-start.10 = (bf16[96,896]{1,0:T(8,128)(2,1)S(1)}, bf16[96,896]{1,0:T(8,128)(2,1)S(1)}, u32[]{:S(2)}, u32[]{:S(2)}) collective-permute-start(bf16[96,896]{1,0:T(8,128)(2,1)S(1)} %collective-permute-done.6.x11.x101), channel_id=1, source_target_pairs={{0,2},{2,0},{4,6},{6,4},{8,10},{10,8},{12,14},{14,12},{16,18},{18,... | collective-permute-start | bytes 516104 | tf_op jit(solution)/shard_map/ppermute | solution.py:331
  27.5 7.1 %collective-permute-start.9 = (bf16[96,896]{1,0:T(8,128)(2,1)S(1)}, bf16[96,896]{1,0:T(8,128)(2,1)S(1)}, u32[]{:S(2)}, u32[]{:S(2)}) collective-permute-start(bf16[96,896]{1,0:T(8,128)(2,1)S(1)} %collective-permute-done.5.x10.x100), channel_id=1, source_target_pairs={{0,2},{2,0},{4,6},{6,4},{8,10},{10,8},{12,14},{14,12},{16,18},{18,... | collective-permute-start | bytes 516104 | tf_op jit(solution)/shard_map/ppermute | solution.py:331
  29.3 5.4 %collective-permute-start.8 = (bf16[96,896]{1,0:T(8,128)(2,1)S(1)}, bf16[96,896]{1,0:T(8,128)(2,1)}, u32[]{:S(2)}, u32[]{:S(2)}) collective-permute-start(bf16[96,896]{1,0:T(8,128)(2,1)S(1)} %collective-permute-done.4.x01.x001), channel_id=1, source_target_pairs={{0,2},{2,0},{4,6},{6,4},{8,10},{10,8},{12,14},{14,12},{16,18},{18,... | collective-permute-start | bytes 516104 | tf_op jit(solution)/shard_map/ppermute | solution.py:331
  36.5 5.3 %collective-permute-start.12 = (bf16[192,256]{1,0:T(8,128)(2,1)S(1)}, bf16[192,256]{1,0:T(8,128)(2,1)S(1)}, u32[]{:S(2)}, u32[]{:S(2)}) collective-permute-start(bf16[192,256]{1,0:T(8,128)(2,1)S(1)} %get-tuple-element.26.own), channel_id=1, source_target_pairs={{0,1},{1,0},{2,3},{3,2},{4,5},{5,4},{6,7},{7,6},{8,9},{9,8},{10,11... | collective-permute-start | bytes 294920 | tf_op jit(solution)/shard_map/ppermute | solution.py:333
  36.8 6.1 %collective-permute-start.18 = (bf16[96,896]{1,0:T(8,128)(2,1)S(1)}, bf16[96,896]{1,0:T(8,128)(2,1)S(1)}, u32[]{:S(2)}, u32[]{:S(2)}) collective-permute-start(bf16[96,896]{1,0:T(8,128)(2,1)S(1)} %slice.187), channel_id=1, source_target_pairs={{0,2},{2,0},{4,6},{6,4},{8,10},{10,8},{12,14},{14,12},{16,18},{18,... | collective-permute-start | bytes 516104 | tf_op jit(solution)/shard_map/ppermute | solution.py:331
  37.2 5.8 %collective-permute-start.19 = (bf16[96,896]{1,0:T(8,128)(2,1)S(1)}, bf16[96,896]{1,0:T(8,128)(2,1)S(1)}, u32[]{:S(2)}, u32[]{:S(2)}) collective-permute-start(bf16[96,896]{1,0:T(8,128)(2,1)S(1)} %slice.188), channel_id=1, source_target_pairs={{0,2},{2,0},{4,6},{6,4},{8,10},{10,8},{12,14},{14,12},{16,18},{18,... | collective-permute-start | bytes 516104 | tf_op jit(solution)/shard_map/ppermute | solution.py:331
  42.9 12.2 %collective-permute-start.13 = (bf16[192,896]{1,0:T(8,128)(2,1)S(1)}, bf16[192,896]{1,0:T(8,128)(2,1)S(1)}, u32[]{:S(2)}, u32[]{:S(2)}) collective-permute-start(bf16[192,896]{1,0:T(8,128)(2,1)S(1)} %get-tuple-element.29), channel_id=1, source_target_pairs={{0,2},{2,0},{4,6},{6,4},{8,10},{10,8},{12,14},{14,12},{16,18},{18,... | collective-permute-start | bytes 1032200 | tf_op jit(solution)/shard_map/ppermute | solution.py:331
  50.7 9.1 %collective-permute-start.21 = (bf16[2,192,896]{2,1,0:T(8,128)(2,1)S(1)}, bf16[2,192,896]{2,1,0:T(8,128)(2,1)S(1)}, u32[]{:S(2)}, u32[]{:S(2)}) collective-permute-start(bf16[2,192,896]{2,1,0:T(8,128)(2,1)S(1)} %get-tuple-element.36), channel_id=1, source_target_pairs={{0,2},{2,0},{4,6},{6,4},{8,10},{10,8},{12,14},{14,12},{16,18},{18,... | collective-permute-start | bytes 2064392 | tf_op jit(solution)/shard_map/ppermute | solution.py:331
  55.2 8.2 %collective-permute-start.15 = (bf16[48,896]{1,0:T(8,128)(2,1)S(1)}, bf16[48,896]{1,0:T(8,128)(2,1)S(1)}, u32[]{:S(2)}, u32[]{:S(2)}) collective-permute-start(bf16[48,896]{1,0:T(8,128)(2,1)S(1)} %pad_maximum_fusion.4), channel_id=1, source_target_pairs={{0,16},{2,18},{4,20},{6,22},{8,24},{10,26},{12,28},{14,30},{16,0},... | collective-permute-start | bytes 258056 | tf_op jit(solution)/shard_map/ppermute | solution.py:331
  55.3 8.4 %collective-permute-start.16 = (bf16[48,896]{1,0:T(8,128)(2,1)S(1)}, bf16[48,896]{1,0:T(8,128)(2,1)S(1)}, u32[]{:S(2)}, u32[]{:S(2)}) collective-permute-start(bf16[48,896]{1,0:T(8,128)(2,1)S(1)} %pad_maximum_fusion.5), channel_id=1, source_target_pairs={{0,8},{2,10},{4,12},{6,14},{8,0},{10,2},{12,4},{14,6},{16,24},{18,... | collective-permute-start | bytes 258056 | tf_op jit(solution)/shard_map/ppermute | solution.py:331
  58.4 6.6 %collective-permute-start.14 = (bf16[48,896]{1,0:T(8,128)(2,1)S(1)}, bf16[48,896]{1,0:T(8,128)(2,1)S(1)}, u32[]{:S(2)}, u32[]{:S(2)}) collective-permute-start(bf16[48,896]{1,0:T(8,128)(2,1)S(1)} %pad_maximum_fusion.3), channel_id=1, source_target_pairs={{0,24},{2,26},{4,28},{6,30},{8,16},{10,18},{12,20},{14,22},{16,8},... | collective-permute-start | bytes 258056 | tf_op jit(solution)/shard_map/ppermute | solution.py:331
  60.1 7.3 %collective-permute-start.22 = (bf16[96,896]{1,0:T(8,128)(2,1)S(1)}, bf16[96,896]{1,0:T(8,128)(2,1)S(1)}, u32[]{:S(2)}, u32[]{:S(2)}) collective-permute-start(bf16[96,896]{1,0:T(8,128)(2,1)S(1)} %get-tuple-element.47), channel_id=1, source_target_pairs={{0,4},{2,6},{4,0},{6,2},{8,12},{10,14},{12,8},{14,10},{16,20},{18,... | collective-permute-start | bytes 516104 | tf_op jit(solution)/shard_map/ppermute | solution.py:331
  61.6 8.4 %collective-permute-start.24 = (bf16[96,896]{1,0:T(8,128)(2,1)S(1)}, bf16[96,896]{1,0:T(8,128)(2,1)S(1)}, u32[]{:S(2)}, u32[]{:S(2)}) collective-permute-start(bf16[96,896]{1,0:T(8,128)(2,1)S(1)} %get-tuple-element.48), channel_id=1, source_target_pairs={{0,5},{1,4},{2,7},{3,6},{4,1},{5,0},{6,3},{7,2},{8,13},{9,12},{10,... | collective-permute-start | bytes 516104 | tf_op jit(solution)/shard_map/ppermute | solution.py:334
  63.4 9.0 %collective-permute-start.23 = (bf16[96,896]{1,0:T(8,128)(2,1)S(1)}, bf16[96,896]{1,0:T(8,128)(2,1)S(1)}, u32[]{:S(2)}, u32[]{:S(2)}) collective-permute-start(bf16[96,896]{1,0:T(8,128)(2,1)S(1)} %get-tuple-element.49), channel_id=1, source_target_pairs={{0,1},{1,0},{2,3},{3,2},{4,5},{5,4},{6,7},{7,6},{8,9},{9,8},{10,11... | collective-permute-start | bytes 516104 | tf_op jit(solution)/shard_map/ppermute | solution.py:333
  65.1 11.8 %collective-permute-start.17 = (bf16[24,896]{1,0:T(8,128)(2,1)S(1)}, bf16[24,896]{1,0:T(8,128)(2,1)S(1)}, u32[]{:S(2)}, u32[]{:S(2)}) collective-permute-start(bf16[24,896]{1,0:T(8,128)(2,1)S(1)} %slice.236), channel_id=1, source_target_pairs={{0,4},{2,6},{4,0},{6,2},{8,12},{10,14},{12,8},{14,10},{16,20},{18,... | collective-permute-start | bytes 129032 | tf_op jit(solution)/shard_map/ppermute | solution.py:331
  72.5 5.9 %collective-permute-start.25 = (bf16[24,896]{1,0:T(8,128)(2,1)S(1)}, bf16[24,896]{1,0:T(8,128)(2,1)S(1)}, u32[]{:S(2)}, u32[]{:S(2)}) collective-permute-start(bf16[24,896]{1,0:T(8,128)(2,1)S(1)} %get-tuple-element.56), channel_id=1, source_target_pairs={{0,24},{2,26},{4,28},{6,30},{8,16},{10,18},{12,20},{14,22},{16,8},... | collective-permute-start | bytes 129032 | tf_op jit(solution)/shard_map/ppermute | solution.py:331
  (8 other events, 49.3 us)
